TPU v7x, 32 devices: a whole 2x2x4 slice. The times are simulated.
32 devices in a mesh: row: 4 (over z), col: 8 (over y, x, core).
Axes of the slice: x: 2, y: 2, z: 4, core: 2. Of those that a mesh axis runs over, the one named last changes fastest.
Arguments:
- pair: bfloat16 [128, 128, 128], P('row', 'col'), may hold values from -6 to 6
- gain_in: float32 [128], replicated, may hold values from 0.1 to 1.9
- w_left_gate: bfloat16 [128, 128], replicated, may hold values from -0.5 to 0.5
- w_left: bfloat16 [128, 128], replicated, may hold values from -0.5 to 0.5
- w_right_gate: bfloat16 [128, 128], replicated, may hold values from -0.5 to 0.5
- w_right: bfloat16 [128, 128], replicated, may hold values from -0.5 to 0.5
- gain_out: float32 [128], replicated, may hold values from 0.1 to 1.9
- w_out_gate: bfloat16 [128, 128], replicated, may hold values from -0.5 to 0.5
- w_out: bfloat16 [128, 128], replicated, may hold values from -0.5 to 0.5
Outputs:
- update: bfloat16 [128, 128, 128], P('row', 'col')
All inputs are finite; a program needn't handle non-finite values.
Results may differ from a plain program's by a relative error of at most 0.0081.
Values may be sent and summed in bfloat16 or wider, within the bound.
A program may use at most 64 MiB of HBM per device.

v0:
```python
import jax
import jax.numpy as jnp
from jax import lax
from jax.sharding import PartitionSpec as P


def spread(value, axis, source):
    kept = jnp.where(lax.axis_index(axis) == source, value, 0).astype(value.dtype)
    return lax.psum(kept, axis)


def layer_norm(values, gain):
    mean = jnp.mean(values, axis=-1, keepdims=True)
    centred = values - mean
    variance = jnp.mean(centred * centred, axis=-1, keepdims=True)
    return centred * lax.rsqrt(variance + 1e-05) * gain


def project(normed, weight):
    return jnp.einsum("ijc,ch->ijh", normed, weight, preferred_element_type=jnp.float32)


def per_device(
    pair, gain_in, w_left_gate, w_left, w_right_gate, w_right, gain_out, w_out_gate, w_out
):
    col_block = pair.shape[1]
    normed = layer_norm(pair.astype(jnp.float32), gain_in).astype(jnp.bfloat16)
    left = (jax.nn.sigmoid(project(normed, w_left_gate)) * project(normed, w_left)).astype(
        jnp.bfloat16
    )
    right = (jax.nn.sigmoid(project(normed, w_right_gate)) * project(normed, w_right)).astype(
        jnp.bfloat16
    )
    panel = lax.all_gather(right, "col", axis=1, tiled=True)
    ratio = lax.axis_size("col") // lax.axis_size("row")
    column = lax.axis_index("col")
    owned = lax.dynamic_slice_in_dim(panel, column % ratio * col_block, col_block, 0)
    right_cols = spread(owned, "row", column // ratio)
    mixed = jnp.einsum(
        "ikh,jkh->ijh",
        lax.all_gather(left, "col", axis=1, tiled=True),
        right_cols,
        preferred_element_type=jnp.float32,
    )
    out_normed = layer_norm(mixed, gain_out).astype(jnp.bfloat16)
    gate = jax.nn.sigmoid(project(normed, w_out_gate))
    return (gate * project(out_normed, w_out)).astype(jnp.bfloat16)


def solution(mesh):
    return jax.shard_map(
        per_device,
        mesh=mesh,
        in_specs=(P("row", "col", None), P(), P(), P(), P(), P(), P(), P(), P()),
        out_specs=P("row", "col", None),
        check_vma=False,
    )
```

profile of v0, /device:TPU:0, one launch (start us, length us, event | category | flops | bytes accessed | tf_op | source)
XLA Modules:
  0.0 118.3 jit_solution(17860925446135129522)
XLA Ops:
  6.5 0.0 copy-start
  6.5 0.0 copy-start.1
  6.5 0.0 copy-start.3
  6.5 0.0 copy-start.5
  6.5 0.0 all-gather.3.cloned.1.call-start
  6.6 1.1 convert_reduce_fusion
  7.7 0.1 copy.27
  7.8 0.1 copy.28
  7.8 1.1 fusion.14
  9.0 0.1 copy.29
  9.1 0.1 copy.30
  9.2 0.0 copy-done
  9.2 1.2 %fusion.5 = f32[32,16,128]{2,1,0:T(8,128)S(1)} fusion(bf16[128,128]{1,0:T(8,128)(2,1)S(1)} %copy-done, bf16[32,16,128]{2,1,0:T(8,128)(2,1)} %param.9, f32[128]{0:T(128)} %param.10, f32[32,16]{1,0:T(8,128)S(1)} %copy.30, f32[32,16]{1,0:T(8,128)S(1)} %copy.28), kind=kOutput, calls=%fused_computation.11 | convolution fusion | flops 17301504 | bytes 430592 | tf_op jit(solution)/shard_map/ijc,ch->ijh/dot_general | solution.py:20
  10.4 1.9 %fusion.9 = bf16[32,16,128]{2,1,0:T(8,128)(2,1)} fusion(f32[32,16,128]{2,1,0:T(8,128)S(1)} %fusion.5, bf16[128,128]{1,0:T(8,128)(2,1)} %param.14, bf16[32,16,128]{2,1,0:T(8,128)(2,1)} %param.9, f32[128]{0:T(128)} %param.10, f32[32,16]{1,0:T(8,128)S(1)} %copy.30, f32[32,16]{1,0:T(8,128)S(1)} %copy.28), kind=kOutput, calls=%fused_computation.16 | convolution fusion | flops 17235968 | bytes 561664 | tf_op jit(solution)/shard_map/ijc,ch->ijh/dot_general | solution.py:20
  12.3 0.0 all-gather.3.cloned.1.call-update
  12.3 0.0 all-gather.5.cloned.1.call-start
  12.4 1.3 %fusion.2 = f32[32,16,128]{2,1,0:T(8,128)S(1)} fusion(bf16[128,128]{1,0:T(8,128)(2,1)} %param.11, bf16[32,16,128]{2,1,0:T(8,128)(2,1)} %param.9, f32[128]{0:T(128)} %param.10, f32[32,16]{1,0:T(8,128)S(1)} %copy.30, f32[32,16]{1,0:T(8,128)S(1)} %copy.28), kind=kOutput, calls=%fused_computation.7 | convolution fusion | flops 17301504 | bytes 430592 | tf_op jit(solution)/shard_map/ijc,ch->ijh/dot_general | solution.py:20
  13.7 1.9 %fusion.10 = bf16[32,16,128]{2,1,0:T(8,128)(2,1)} fusion(f32[32,16,128]{2,1,0:T(8,128)S(1)} %fusion.2, bf16[128,128]{1,0:T(8,128)(2,1)} %param.12, bf16[32,16,128]{2,1,0:T(8,128)(2,1)} %param.9, f32[128]{0:T(128)} %param.10, f32[32,16]{1,0:T(8,128)S(1)} %copy.30, f32[32,16]{1,0:T(8,128)S(1)} %copy.28), kind=kOutput, calls=%fused_computation.17 | convolution fusion | flops 17235968 | bytes 561664 | tf_op jit(solution)/shard_map/ijc,ch->ijh/dot_general | solution.py:20
  15.6 0.0 all-gather.5.cloned.1.call-update
  15.6 0.0 all-reduce.2.cloned.1.call-start
  15.7 23.1 %all-gather.3.cloned.1.call-done = bf16[32,128,128]{2,1,0:T(8,128)(2,1)} async-done(((bf16[32,16,128]{2,1,0:T(8,128)(2,1)}), bf16[32,128,128]{2,1,0:T(8,128)(2,1)}) %all-gather.3.cloned.1.call-update) | async-done | bytes 1048592 | tf_op jit(solution)/shard_map/all_gather | solution.py:34
  38.7 1.9 %dynamic-slice_select_fusion = bf16[16,128,128]{2,1,0:T(8,128)(2,1)} fusion(bf16[32,128,128]{2,1,0:T(8,128)(2,1)} %all-gather.3.cloned.1.call-done, s32[]{:T(128)S(6)} %select_n.25, pred[]{:T(512)S(6)} %eq.5), kind=kLoop, calls=%fused_computation.21 | loop fusion | flops 262144 | bytes 1048581 | tf_op jit(solution)/shard_map/jit(_where)/select_n | solution.py:8
  40.6 0.0 all-reduce.2.cloned.1.call-update
  40.6 0.0 copy-done.1
  40.6 0.0 copy-done.3
  40.6 0.0 copy-done.5
  40.6 0.3 fusion.8
  41.0 23.1 %all-gather.5.cloned.1.call-done = bf16[32,128,128]{2,1,0:T(8,128)(2,1)} async-done(((bf16[32,16,128]{2,1,0:T(8,128)(2,1)}), bf16[32,128,128]{2,1,0:T(8,128)(2,1)}) %all-gather.5.cloned.1.call-update) | async-done | bytes 1048592 | tf_op jit(solution)/shard_map/all_gather | solution.py:41
  64.1 8.6 %copy.32 = bf16[32,128,128]{0,1,2:T(8,128)(2,1)} copy(bf16[32,128,128]{2,1,0:T(8,128)(2,1)} %all-gather.5.cloned.1.call-done) | data formatting | bytes 2097152 | tf_op jit(solution)/shard_map/all_gather | solution.py:41
  72.7 0.0 copy-start.4
  72.7 32.4 %all-reduce.2.cloned.1.call-done = bf16[16,128,128]{2,1,0:T(8,128)(2,1)} async-done(((bf16[16,128,128]{2,1,0:T(8,128)(2,1)}), bf16[16,128,128]{2,1,0:T(8,128)(2,1)}) %all-reduce.2.cloned.1.call-update) | async-done | bytes 524304 | tf_op jit(solution)/shard_map/psum | solution.py:9
  105.1 1.5 %copy.31 = bf16[16,128,128]{1,0,2:T(8,128)(2,1)S(1)} copy(bf16[16,128,128]{2,1,0:T(8,128)(2,1)} %all-reduce.2.cloned.1.call-done) | data formatting | bytes 1048576 | tf_op jit(solution)/shard_map/psum | solution.py:9
  106.6 0.0 copy-start.2
  106.6 3.4 %fusion.28 = (f32[32,16]{0,1:T(8,128)S(1)}, f32[32,16,128]{0,1,2:T(8,128)S(1)}) fusion(bf16[16,128,128]{1,0,2:T(8,128)(2,1)S(1)} %copy.31, bf16[32,128,128]{0,1,2:T(8,128)(2,1)} %copy.32), kind=kOutput, calls=%fused_computation.39 | convolution fusion | flops 16842240 | bytes 1837056 | tf_op jit(solution)/shard_map/ikh,jkh->ijh/dot_general | solution.py:39
  110.0 0.2 multiply_reduce_fusion
  110.2 0.0 copy-done.4
  110.2 0.2 multiply_convert_fusion
  110.4 0.5 copy.33
  110.9 0.0 copy-done.2
  110.9 0.8 fusion.11
  (4 shorter events, 0.0 us)
Async XLA Ops:
  6.5 2.6 %copy-start = (bf16[128,128]{1,0:T(8,128)(2,1)S(1)}, bf16[128,128]{1,0:T(8,128)(2,1)}, u32[]{:S(2)}) copy-start(bf16[128,128]{1,0:T(8,128)(2,1)} %param.13) | copy-start | bytes 98308
  6.5 34.1 %copy-start.1 = (bf16[32,16,128]{2,1,0:T(8,128)(2,1)S(1)}, bf16[32,16,128]{2,1,0:T(8,128)(2,1)}, u32[]{:S(2)}) copy-start(bf16[32,16,128]{2,1,0:T(8,128)(2,1)} %param.9) | copy-start | bytes 393220
  6.5 34.1 %copy-start.3 = (f32[128]{0:T(128)S(1)}, f32[128]{0:T(128)}, u32[]{:S(2)}) copy-start(f32[128]{0:T(128)} %param.10) | copy-start | bytes 1540
  6.5 34.1 %copy-start.5 = (bf16[128,128]{1,0:T(8,128)(2,1)S(1)}, bf16[128,128]{1,0:T(8,128)(2,1)}, u32[]{:S(2)}) copy-start(bf16[128,128]{1,0:T(8,128)(2,1)} %param.16) | copy-start | bytes 98308
  6.5 32.2 %all-gather.3.cloned.1.call-start = ((), (), s32[]{:S(2)}) async-start(), calls=%async_computation | async-start | bytes 1179648 | tf_op jit(solution)/shard_map/all_gather | solution.py:34
  12.3 51.7 %all-gather.5.cloned.1.call-start = ((), (), s32[]{:S(2)}) async-start(), calls=%async_computation.2 | async-start | bytes 1179648 | tf_op jit(solution)/shard_map/all_gather | solution.py:41
  15.6 89.5 %all-reduce.2.cloned.1.call-start = ((), (), s32[]{:S(2)}) async-start(), calls=%async_computation.1 | async-start | bytes 1048576 | tf_op jit(solution)/shard_map/psum | solution.py:9
  72.7 37.5 %copy-start.4 = (f32[128]{0:T(128)S(1)}, f32[128]{0:T(128)}, u32[]{:S(2)}) copy-start(f32[128]{0:T(128)} %param.15) | copy-start | bytes 1540
  106.6 4.4 %copy-start.2 = (bf16[128,128]{1,0:T(8,128)(2,1)S(1)}, bf16[128,128]{1,0:T(8,128)(2,1)}, u32[]{:S(2)}) copy-start(bf16[128,128]{1,0:T(8,128)(2,1)} %param.17) | copy-start | bytes 98308
Sparse Core Ops, SparseCore 0:
  12.5 26.1 all-gather.2
  40.6 23.4 all-gather.4
  66.4 38.6 all-reduce.1
where the time goes:
time: 119 us; the launch traced here: 118 us
  waiting for transfers between devices  78.6 us (66%)
  between operations  13.3 us (11%)
  local copies, waits for them, and re-layouts  10.9 us (9%)
  matrix products  10.9 us (9%)
  other arithmetic  4.59 us (4%)
    psum x1, waiting for transfers between devices, spread(): return lax.psum(kept, axis)  32.4 us
    all_gather x1, waiting for transfers between devices, per_device(): lax.all_gather(left, 'col', axis=1, tiled=True)  23.1 us
    all_gather x1, waiting for transfers between devices, per_device(): panel = lax.all_gather(right, 'col', axis=1, tiled=True)  23.1 us
    all_gather x1, local copies, waits for them, and re-layouts, per_device(): lax.all_gather(left, 'col', axis=1, tiled=True)  8.61 us
    dot_general x6, matrix products, project(): jnp.einsum('ijc,ch->ijh', normed, weight, preferred_element_type=jnp.floa...  7.46 us
    dot_general x1, matrix products, per_device(): jnp.einsum('ikh,jkh->ijh', lax.all_gather(left, 'col', axis=1, tiled=True...  3.39 us
  transfers between devices with their start and end apart: 3, of which 3 were waited for; matrix products, arithmetic and copies ran while one was open for 12% of the time, Pallas kernels for 0%

commit v1 on v0

--- a/solution.py
+++ b/solution.py
@@ -31,7 +31,12 @@
     right = (jax.nn.sigmoid(project(normed, w_right_gate)) * project(normed, w_right)).astype(
         jnp.bfloat16
     )
-    panel = lax.all_gather(right, "col", axis=1, tiled=True)
+    ring = [right]
+    for hop in range(7):
+        ring.append(lax.ppermute(ring[-1], "col", [(dev, (dev + 1) % 8) for dev in range(8)]))
+    panel = jnp.roll(
+        jnp.concatenate(ring[::-1], axis=1), (lax.axis_index("col") + 1) * ring[0].shape[1], axis=1
+    )
     ratio = lax.axis_size("col") // lax.axis_size("row")
     column = lax.axis_index("col")
     owned = lax.dynamic_slice_in_dim(panel, column % ratio * col_block, col_block, 0)

time: 119 us -> 115 us (0.966)
  waiting for transfers between devices: 78.6 us -> 75.3 us
  matrix products: 10.9 us -> 8.36 us
  between operations: 13.3 us -> 15.1 us
    ppermute x0 -> x7, waiting for transfers between devices: none -> 37.3 us  [per_device(): lax.ppermute(ring[-1], 'col', [(dev, (dev + 1) % 8) for dev in range(8)])]
    all_gather x1, waiting for transfers between devices: 23.1 us -> 0.03 us  [per_device(): lax.all_gather(left, 'col', axis=1, tiled=True)]
    all_gather x1 -> x0, waiting for transfers between devices: 23.1 us -> none  [per_device(): panel = lax.all_gather(right, 'col', axis=1, tiled=True)]
    psum x1, waiting for transfers between devices: 32.4 us -> 37.9 us  [spread(): return lax.psum(kept, axis)]
    dot_general x6, matrix products: 7.46 us -> 4.96 us  [project(): jnp.einsum('ijc,ch->ijh', normed, weight, preferred_element_type=jnp.floa...]
  transfers between devices with their start and end apart: 3 -> 9, of which waited for: 3 -> 8; matrix products, arithmetic and copies ran while one was open for 12% -> 3% of each run, Pallas kernels for 0% -> 0%
where the time goes in v1:
time: 115 us; the launch traced here: 114 us
  waiting for transfers between devices  75.3 us (65%)
  between operations  15.1 us (13%)
  local copies, waits for them, and re-layouts  11.2 us (10%)
  matrix products  8.36 us (7%)
  other arithmetic  3.64 us (3%)
    psum x1, waiting for transfers between devices, spread(): return lax.psum(kept, axis)  37.9 us
    ppermute x7, waiting for transfers between devices, per_device(): lax.ppermute(ring[-1], 'col', [(dev, (dev + 1) % 8) for dev in range(8)])  37.3 us
    all_gather x1, local copies, waits for them, and re-layouts, per_device(): lax.all_gather(left, 'col', axis=1, tiled=True)  8.63 us
    dot_general x6, matrix products, project(): jnp.einsum('ijc,ch->ijh', normed, weight, preferred_element_type=jnp.floa...  4.96 us
    dot_general x1, matrix products, per_device(): jnp.einsum('ikh,jkh->ijh', lax.all_gather(left, 'col', axis=1, tiled=True...  3.4 us
  transfers between devices with their start and end apart: 9, of which 8 were waited for; matrix products, arithmetic and copies ran while one was open for 3% of the time, Pallas kernels for 0%

profile of v1, /device:TPU:0, one launch (start us, length us, event | category | flops | bytes accessed | tf_op | source)
XLA Modules:
  0.0 114.2 jit_solution(3714377287982830165)
XLA Ops:
  7.4 0.0 copy-start
  7.4 0.0 all-reduce.2.cloned.1.call-start
  7.4 1.1 convert_reduce_fusion
  8.4 0.1 copy.27
  8.5 0.1 copy.28
  8.6 1.1 %fusion.14 = f32[32,16]{1,0:T(8,128)S(1)} fusion(bf16[32,16,128]{2,1,0:T(8,128)(2,1)} %param.9, f32[32,16]{1,0:T(8,128)S(1)} %copy.28), kind=kLoop, calls=%fused_computation.26 | loop fusion | flops 261632 | bytes 135168 | tf_op jit(solution)/shard_map/reduce_sum | solution.py:15
  9.7 0.1 copy.29
  9.8 0.1 copy.30
  9.9 0.0 copy-done
  9.9 1.2 %fusion.5 = f32[32,16,128]{2,1,0:T(8,128)S(1)} fusion(bf16[128,128]{1,0:T(8,128)(2,1)S(1)} %copy-done, bf16[32,16,128]{2,1,0:T(8,128)(2,1)} %param.9, f32[128]{0:T(128)} %param.10, f32[32,16]{1,0:T(8,128)S(1)} %copy.30, f32[32,16]{1,0:T(8,128)S(1)} %copy.28), kind=kOutput, calls=%fused_computation.11 | convolution fusion | flops 17301504 | bytes 430592 | tf_op jit(solution)/shard_map/ijc,ch->ijh/dot_general | solution.py:20
  11.2 1.2 %fusion.9 = bf16[32,16,128]{2,1,0:T(8,128)(2,1)S(1)} fusion(f32[32,16,128]{2,1,0:T(8,128)S(1)} %fusion.5, bf16[128,128]{1,0:T(8,128)(2,1)} %param.14, bf16[32,16,128]{2,1,0:T(8,128)(2,1)} %param.9, f32[128]{0:T(128)} %param.10, f32[32,16]{1,0:T(8,128)S(1)} %copy.30, f32[32,16]{1,0:T(8,128)S(1)} %copy.28), kind=kOutput, calls=%fused_computation.16 | convolution fusion | flops 17235968 | bytes 561664 | tf_op jit(solution)/shard_map/ijc,ch->ijh/dot_general | solution.py:20
  12.4 0.5 collective-permute-start
  12.9 5.5 %collective-permute-done = bf16[32,16,128]{2,1,0:T(8,128)(2,1)S(1)} collective-permute-done((bf16[32,16,128]{2,1,0:T(8,128)(2,1)S(1)}, bf16[32,16,128]{2,1,0:T(8,128)(2,1)S(1)}, u32[]{:S(2)}, u32[]{:S(2)}) %collective-permute-start) | collective-permute-done | bytes 131104 | tf_op jit(solution)/shard_map/ppermute | solution.py:36
  18.5 0.0 collective-permute-start.1
  18.5 5.3 %collective-permute-done.1 = bf16[32,16,128]{2,1,0:T(8,128)(2,1)S(1)} collective-permute-done((bf16[32,16,128]{2,1,0:T(8,128)(2,1)S(1)}, bf16[32,16,128]{2,1,0:T(8,128)(2,1)S(1)}, u32[]{:S(2)}, u32[]{:S(2)}) %collective-permute-start.1) | collective-permute-done | bytes 131104 | tf_op jit(solution)/shard_map/ppermute | solution.py:36
  23.8 0.0 collective-permute-start.2
  23.8 5.3 %collective-permute-done.2 = bf16[32,16,128]{2,1,0:T(8,128)(2,1)S(1)} collective-permute-done((bf16[32,16,128]{2,1,0:T(8,128)(2,1)S(1)}, bf16[32,16,128]{2,1,0:T(8,128)(2,1)S(1)}, u32[]{:S(2)}, u32[]{:S(2)}) %collective-permute-start.2) | collective-permute-done | bytes 131104 | tf_op jit(solution)/shard_map/ppermute | solution.py:36
  29.0 0.0 collective-permute-start.3
  29.1 5.3 %collective-permute-done.3 = bf16[32,16,128]{2,1,0:T(8,128)(2,1)S(1)} collective-permute-done((bf16[32,16,128]{2,1,0:T(8,128)(2,1)S(1)}, bf16[32,16,128]{2,1,0:T(8,128)(2,1)S(1)}, u32[]{:S(2)}, u32[]{:S(2)}) %collective-permute-start.3) | collective-permute-done | bytes 131104 | tf_op jit(solution)/shard_map/ppermute | solution.py:36
  34.3 0.0 collective-permute-start.4
  34.3 5.3 %collective-permute-done.4 = bf16[32,16,128]{2,1,0:T(8,128)(2,1)S(1)} collective-permute-done((bf16[32,16,128]{2,1,0:T(8,128)(2,1)S(1)}, bf16[32,16,128]{2,1,0:T(8,128)(2,1)S(1)}, u32[]{:S(2)}, u32[]{:S(2)}) %collective-permute-start.4) | collective-permute-done | bytes 131104 | tf_op jit(solution)/shard_map/ppermute | solution.py:36
  39.6 0.0 collective-permute-start.5
  39.6 5.3 %collective-permute-done.5 = bf16[32,16,128]{2,1,0:T(8,128)(2,1)S(1)} collective-permute-done((bf16[32,16,128]{2,1,0:T(8,128)(2,1)S(1)}, bf16[32,16,128]{2,1,0:T(8,128)(2,1)S(1)}, u32[]{:S(2)}, u32[]{:S(2)}) %collective-permute-start.5) | collective-permute-done | bytes 131104 | tf_op jit(solution)/shard_map/ppermute | solution.py:36
  44.9 0.0 collective-permute-start.6
  44.9 5.3 %collective-permute-done.6 = bf16[32,16,128]{2,1,0:T(8,128)(2,1)S(1)} collective-permute-done((bf16[32,16,128]{2,1,0:T(8,128)(2,1)S(1)}, bf16[32,16,128]{2,1,0:T(8,128)(2,1)S(1)}, u32[]{:S(2)}, u32[]{:S(2)}) %collective-permute-start.6) | collective-permute-done | bytes 131104 | tf_op jit(solution)/shard_map/ppermute | solution.py:36
  50.4 0.0 copy-start.1
  50.4 0.0 copy-start.4
  50.4 0.0 copy-start.6
  50.6 0.0 copy-start.3
  50.6 0.0 copy-start.7
  50.7 1.0 dynamic-slice_select_fusion
  51.7 0.0 all-reduce.2.cloned.1.call-update
  51.7 0.0 all-gather.2.cloned.1.call-start
  51.8 0.0 copy-done.1
  51.8 0.0 copy-done.4
  51.8 0.0 copy-done.6
  51.8 0.3 fusion.2
  52.1 0.0 copy-done.3
  52.2 1.0 fusion.10
  53.1 0.0 all-gather.2.cloned.1.call-update
  53.2 0.0 copy-done.7
  53.2 0.3 fusion.8
  53.5 37.9 %all-reduce.2.cloned.1.call-done = bf16[16,128,128]{2,1,0:T(8,128)(2,1)} async-done(((bf16[16,128,128]{2,1,0:T(8,128)(2,1)}), bf16[16,128,128]{2,1,0:T(8,128)(2,1)}) %all-reduce.2.cloned.1.call-update) | async-done | bytes 524304 | tf_op jit(solution)/shard_map/psum | solution.py:9
  91.5 1.5 %copy.31 = bf16[16,128,128]{1,0,2:T(8,128)(2,1)S(1)} copy(bf16[16,128,128]{2,1,0:T(8,128)(2,1)} %all-reduce.2.cloned.1.call-done) | data formatting | bytes 1048576 | tf_op jit(solution)/shard_map/psum | solution.py:9
  92.9 0.0 all-gather.2.cloned.1.call-done
  93.0 8.6 %copy.32 = bf16[32,128,128]{0,1,2:T(8,128)(2,1)} copy(bf16[32,128,128]{2,1,0:T(8,128)(2,1)} %all-gather.2.cloned.1.call-done) | data formatting | bytes 2097152 | tf_op jit(solution)/shard_map/all_gather | solution.py:46
  101.6 0.0 copy-start.5
  101.6 3.4 %fusion.28 = (f32[32,16]{0,1:T(8,128)S(1)}, f32[32,16,128]{0,1,2:T(8,128)S(1)}) fusion(bf16[16,128,128]{1,0,2:T(8,128)(2,1)S(1)} %copy.31, bf16[32,128,128]{0,1,2:T(8,128)(2,1)} %copy.32), kind=kOutput, calls=%fused_computation.55 | convolution fusion | flops 16842240 | bytes 1837056 | tf_op jit(solution)/shard_map/ikh,jkh->ijh/dot_general | solution.py:44
  105.0 0.0 copy-start.2
  105.0 0.2 multiply_reduce_fusion
  105.2 0.0 copy-done.5
  105.2 0.2 multiply_convert_fusion
  105.5 0.5 copy.33
  106.0 0.0 copy-done.2
  106.0 0.8 fusion.11
  (20 shorter events, 0.3 us)
Async XLA Ops:
  7.4 2.5 %copy-start = (bf16[128,128]{1,0:T(8,128)(2,1)S(1)}, bf16[128,128]{1,0:T(8,128)(2,1)}, u32[]{:S(2)}) copy-start(bf16[128,128]{1,0:T(8,128)(2,1)} %param.13) | copy-start | bytes 98308
  7.4 84.1 %all-reduce.2.cloned.1.call-start = ((), (), s32[]{:S(2)}) async-start(), calls=%async_computation | async-start | bytes 1048576 | tf_op jit(solution)/shard_map/psum | solution.py:9
  12.4 6.1 %collective-permute-start = (bf16[32,16,128]{2,1,0:T(8,128)(2,1)S(1)}, bf16[32,16,128]{2,1,0:T(8,128)(2,1)S(1)}, u32[]{:S(2)}, u32[]{:S(2)}) collective-permute-start(bf16[32,16,128]{2,1,0:T(8,128)(2,1)S(1)} %fusion.9), channel_id=1, source_target_pairs={{0,1},{1,2},{2,3},{3,4},{4,5},{5,6},{6,7},{7,0},{8,9},{9,10},{10,1... | collective-permute-start | bytes 393224 | tf_op jit(solution)/shard_map/ppermute | solution.py:36
  18.5 5.3 %collective-permute-start.1 = (bf16[32,16,128]{2,1,0:T(8,128)(2,1)S(1)}, bf16[32,16,128]{2,1,0:T(8,128)(2,1)S(1)}, u32[]{:S(2)}, u32[]{:S(2)}) collective-permute-start(bf16[32,16,128]{2,1,0:T(8,128)(2,1)S(1)} %collective-permute-done), channel_id=1, source_target_pairs={{0,1},{1,2},{2,3},{3,4},{4,5},{5,6},{6,7},{7,0},{8,9},{9,10},{10,1... | collective-permute-start | bytes 393224 | tf_op jit(solution)/shard_map/ppermute | solution.py:36
  23.8 5.3 %collective-permute-start.2 = (bf16[32,16,128]{2,1,0:T(8,128)(2,1)S(1)}, bf16[32,16,128]{2,1,0:T(8,128)(2,1)S(1)}, u32[]{:S(2)}, u32[]{:S(2)}) collective-permute-start(bf16[32,16,128]{2,1,0:T(8,128)(2,1)S(1)} %collective-permute-done.1), channel_id=1, source_target_pairs={{0,1},{1,2},{2,3},{3,4},{4,5},{5,6},{6,7},{7,0},{8,9},{9,10},{10,1... | collective-permute-start | bytes 393224 | tf_op jit(solution)/shard_map/ppermute | solution.py:36
  29.0 5.3 %collective-permute-start.3 = (bf16[32,16,128]{2,1,0:T(8,128)(2,1)S(1)}, bf16[32,16,128]{2,1,0:T(8,128)(2,1)S(1)}, u32[]{:S(2)}, u32[]{:S(2)}) collective-permute-start(bf16[32,16,128]{2,1,0:T(8,128)(2,1)S(1)} %collective-permute-done.2), channel_id=1, source_target_pairs={{0,1},{1,2},{2,3},{3,4},{4,5},{5,6},{6,7},{7,0},{8,9},{9,10},{10,1... | collective-permute-start | bytes 393224 | tf_op jit(solution)/shard_map/ppermute | solution.py:36
  34.3 5.3 %collective-permute-start.4 = (bf16[32,16,128]{2,1,0:T(8,128)(2,1)S(1)}, bf16[32,16,128]{2,1,0:T(8,128)(2,1)S(1)}, u32[]{:S(2)}, u32[]{:S(2)}) collective-permute-start(bf16[32,16,128]{2,1,0:T(8,128)(2,1)S(1)} %collective-permute-done.3), channel_id=1, source_target_pairs={{0,1},{1,2},{2,3},{3,4},{4,5},{5,6},{6,7},{7,0},{8,9},{9,10},{10,1... | collective-permute-start | bytes 393224 | tf_op jit(solution)/shard_map/ppermute | solution.py:36
  39.6 5.3 %collective-permute-start.5 = (bf16[32,16,128]{2,1,0:T(8,128)(2,1)S(1)}, bf16[32,16,128]{2,1,0:T(8,128)(2,1)S(1)}, u32[]{:S(2)}, u32[]{:S(2)}) collective-permute-start(bf16[32,16,128]{2,1,0:T(8,128)(2,1)S(1)} %collective-permute-done.4), channel_id=1, source_target_pairs={{0,1},{1,2},{2,3},{3,4},{4,5},{5,6},{6,7},{7,0},{8,9},{9,10},{10,1... | collective-permute-start | bytes 393224 | tf_op jit(solution)/shard_map/ppermute | solution.py:36
  44.9 5.3 %collective-permute-start.6 = (bf16[32,16,128]{2,1,0:T(8,128)(2,1)S(1)}, bf16[32,16,128]{2,1,0:T(8,128)(2,1)S(1)}, u32[]{:S(2)}, u32[]{:S(2)}) collective-permute-start(bf16[32,16,128]{2,1,0:T(8,128)(2,1)S(1)} %collective-permute-done.5), channel_id=1, source_target_pairs={{0,1},{1,2},{2,3},{3,4},{4,5},{5,6},{6,7},{7,0},{8,9},{9,10},{10,1... | collective-permute-start | bytes 393224 | tf_op jit(solution)/shard_map/ppermute | solution.py:36
  50.4 1.4 %copy-start.1 = (bf16[32,16,128]{2,1,0:T(8,128)(2,1)S(1)}, bf16[32,16,128]{2,1,0:T(8,128)(2,1)}, u32[]{:S(2)}) copy-start(bf16[32,16,128]{2,1,0:T(8,128)(2,1)} %param.9) | copy-start | bytes 393220
  50.4 1.4 %copy-start.4 = (f32[128]{0:T(128)S(1)}, f32[128]{0:T(128)}, u32[]{:S(2)}) copy-start(f32[128]{0:T(128)} %param.10) | copy-start | bytes 1540
  50.4 1.4 %copy-start.6 = (bf16[128,128]{1,0:T(8,128)(2,1)S(1)}, bf16[128,128]{1,0:T(8,128)(2,1)}, u32[]{:S(2)}) copy-start(bf16[128,128]{1,0:T(8,128)(2,1)} %param.11) | copy-start | bytes 98308
  50.6 1.6 %copy-start.3 = (bf16[128,128]{1,0:T(8,128)(2,1)S(1)}, bf16[128,128]{1,0:T(8,128)(2,1)}, u32[]{:S(2)}) copy-start(bf16[128,128]{1,0:T(8,128)(2,1)} %param.12) | copy-start | bytes 98308
  50.6 2.5 %copy-start.7 = (bf16[128,128]{1,0:T(8,128)(2,1)S(1)}, bf16[128,128]{1,0:T(8,128)(2,1)}, u32[]{:S(2)}) copy-start(bf16[128,128]{1,0:T(8,128)(2,1)} %param.16) | copy-start | bytes 98308
  51.7 41.2 %all-gather.2.cloned.1.call-start = ((), (), s32[]{:S(2)}) async-start(), calls=%async_computation.1 | async-start | bytes 1179648 | tf_op jit(solution)/shard_map/all_gather | solution.py:46
  101.6 3.6 %copy-start.5 = (f32[128]{0:T(128)S(1)}, f32[128]{0:T(128)}, u32[]{:S(2)}) copy-start(f32[128]{0:T(128)} %param.15) | copy-start | bytes 1540
  105.0 1.0 copy-start.2
Sparse Core Ops, SparseCore 0:
  51.8 39.5 all-reduce.1
Sparse Core Ops, SparseCore 1:
  54.1 24.4 all-gather.1
